TPU v7x, 32 devices: a whole 2x2x4 slice. The times are simulated.
32 devices in a mesh: seq: 4 (over y, core), fsdp: 2 (over x), dp: 4 (over z).
Axes of the slice: x: 2, y: 2, z: 4, core: 2. Of those that a mesh axis runs over, the one named last changes fastest.
Arguments:
- queries: bfloat16 [8, 1024, 4096], P(('fsdp', 'dp'), 'seq'), may hold values from -160 to 160
- hidden: bfloat16 [8, 1024, 8192], P(('fsdp', 'dp'), 'seq'), may hold values from -8 to 8
- key_weight: bfloat16 [8192, 512], P('fsdp'), may hold values from -1 to 1
- doc_lengths: int32 [8, 8], P(('fsdp', 'dp')), may hold values from 1 to 256, 1024 in all within a row
- entropy_cot: bfloat16 [8, 1024, 32], P(('fsdp', 'dp'), 'seq'), may hold values from -600 to 600
Outputs:
- entropy: float32 [8, 1024, 32], P(('fsdp', 'dp'), 'seq')
- grad_queries: bfloat16 [8, 1024, 4096], P(('fsdp', 'dp'), 'seq')
- grad_key_weight: bfloat16 [8192, 512], P('fsdp')
Inputs may be any that keep to these rules, and one draw needn't show every extreme that they name: `doc_lengths`: each sequence's 8 documents are packed in order, their lengths sum to 1024, and the longest is exactly 256.
All inputs are finite; a program needn't handle non-finite values.
Results may differ from a plain program's by a relative error of at most 0.0088.
Values may be sent and summed in bfloat16 or wider, within the bound.
A program may use at most 128 MiB of HBM per device.

v0:
```python
import jax
import jax.numpy as jnp
from jax import lax
from jax.sharding import PartitionSpec as P

QH = 32
KVH = 4
HD = 128


def from_behind(shard, axis, by):
    length = lax.axis_size(axis)
    pairs = [(i, i + by) for i in range(length) if 0 <= i + by < length]
    return lax.ppermute(shard, axis, pairs)


def document_index(lengths, seq_len):
    ends = jnp.cumsum(lengths)
    position = jnp.arange(seq_len, dtype=jnp.int32)
    return jnp.sum((ends[None, :] <= position[:, None]).astype(jnp.int32), axis=1)


def attend(queries, key_rows, cotangent, doc_index, anchor, doc_len):
    row_count, key_heads, group_size, head_size = queries.shape
    full_len = key_rows.shape[0]
    block_rows = min(512, row_count)
    window = block_rows + doc_len
    factor = head_size ** (-0.5)
    keys_padded = jnp.concatenate(
        [jnp.zeros((doc_len, key_heads, head_size), key_rows.dtype), key_rows], axis=0
    )
    index_padded = jnp.concatenate([jnp.full((doc_len,), -1, jnp.int32), doc_index], axis=0)

    def one_block(step_index, state_now):
        entropy, grad_query, grad_key = state_now
        row_start = (step_index * block_rows).astype(jnp.int32)
        position = anchor + row_start
        weight_block = cotangent.astype(jnp.float32)
        key_block = lax.dynamic_slice_in_dim(keys_padded, position, window, 0)
        key_docs = lax.dynamic_slice_in_dim(index_padded, position, window, 0)
        query_docs = lax.dynamic_slice_in_dim(doc_index, position, block_rows, 0)
        query_pos = position + jnp.arange(block_rows, dtype=jnp.int32)
        key_pos = position - doc_len + jnp.arange(window, dtype=jnp.int32)
        visible = (query_docs[:, None] == key_docs[None, :]) & (
            key_pos[None, :] <= query_pos[:, None]
        )
        scores = (
            jnp.einsum("rkgd,wkd->kgrw", queries, key_block, preferred_element_type=jnp.float32)
            * factor
        )
        scores = jnp.where(visible, scores, -1e30)
        row_max = jnp.max(scores, axis=-1, keepdims=True)
        powers = jnp.exp(scores - row_max)
        denominator = jnp.sum(powers, axis=-1, keepdims=True)
        probability = powers / denominator
        mean_score = jnp.sum(jnp.where(visible, probability * scores, 0.0), axis=-1, keepdims=True)
        block_entropy = (row_max + jnp.log(denominator) - mean_score)[..., 0]
        row_weight = jnp.transpose(weight_block, (1, 2, 0))[..., None]
        slope = jnp.where(visible, row_weight * probability * (mean_score - scores), 0.0).astype(
            jnp.bfloat16
        )
        query_part = (
            jnp.einsum("kgrw,wkd->rkgd", slope, key_block, preferred_element_type=jnp.float32)
            * factor
        )
        key_part = (
            jnp.einsum("kgrw,rkgd->wkd", slope, queries, preferred_element_type=jnp.float32)
            * factor
        )
        entropy = jnp.transpose(block_entropy, (2, 0, 1))
        grad_query = query_part
        previous = lax.dynamic_slice_in_dim(grad_key, position, window, 0)
        grad_key = lax.dynamic_update_slice_in_dim(grad_key, previous + key_part, position, 0)
        return (entropy, grad_query, grad_key)

    initial = (
        jnp.zeros((row_count, key_heads, group_size), jnp.float32),
        jnp.zeros((row_count, key_heads, group_size, head_size), jnp.float32),
        jnp.zeros((full_len + doc_len, key_heads, head_size), jnp.float32),
    )
    entropy, grad_query, grad_key = lax.fori_loop(0, row_count // block_rows, one_block, initial)
    return (entropy, grad_query, grad_key[doc_len:])


def per_head(query_four, key_rows, cot_three, doc_index, anchor, doc_len):
    outcome = [
        attend(
            query_four[:, head_index : head_index + 1],
            key_rows[:, head_index : head_index + 1],
            cot_three[:, head_index : head_index + 1],
            doc_index,
            anchor,
            doc_len,
        )
        for head_index in range(query_four.shape[1])
    ]
    entropy = jnp.concatenate([item_set[0] for item_set in outcome], axis=1)
    grad_query = jnp.concatenate([item_set[1] for item_set in outcome], axis=1)
    grad_key = jnp.concatenate([item_set[2] for item_set in outcome], axis=1)
    return (entropy, grad_query, grad_key)


def shards(queries, hidden, key_weight, doc_lengths, entropy_cot):
    tokens = hidden[0]
    local_rows = tokens.shape[0]
    seq_parts = lax.axis_size("seq")
    seq_len = local_rows * seq_parts
    group_size = QH // KVH
    doc_index = document_index(doc_lengths[0], seq_len)
    columns = tokens
    key_local = jnp.dot(
        columns,
        lax.all_gather(key_weight, "fsdp", axis=0, tiled=True),
        preferred_element_type=jnp.float32,
    ).astype(jnp.bfloat16)
    query_local = queries[0]
    cot_local = entropy_cot[0]
    key_prev = from_behind(key_local, "seq", 1)
    device_pos = lax.axis_index("seq")
    start = device_pos * local_rows
    prev_index = lax.dynamic_slice_in_dim(
        doc_index, jnp.maximum(start - local_rows, 0), local_rows, 0
    )
    prev_index = jnp.where(device_pos > 0, prev_index, -1)
    own_index = lax.dynamic_slice_in_dim(doc_index, start, local_rows, 0)
    ext_index = jnp.concatenate([prev_index, own_index], axis=0)
    ext_keys = jnp.concatenate([key_prev, key_local], axis=0).reshape(2 * local_rows, KVH, HD)
    entropy_heads, grad_heads, key_heads_ext = per_head(
        query_local.reshape(local_rows, KVH, group_size, HD),
        ext_keys,
        cot_local.reshape(local_rows, KVH, group_size),
        ext_index,
        local_rows,
        local_rows,
    )
    entropy_local = entropy_heads.reshape(local_rows, QH)
    grad_local = grad_heads.reshape(local_rows, QH * HD)
    key_ext = key_heads_ext.reshape(2 * local_rows, KVH * HD)
    returned = from_behind(key_ext[:local_rows], "seq", -1)
    key_grad = key_ext[local_rows:] + returned
    key_grad_low = key_grad.astype(jnp.bfloat16)
    columns = tokens
    term_rows = lax.psum_scatter(
        lax.dot_general(
            columns, key_grad_low, (((0,), (0,)), ((), ())), preferred_element_type=jnp.float32
        ),
        "fsdp",
        scatter_dimension=0,
        tiled=True,
    )
    summed = lax.psum(term_rows, ("seq", "dp"))
    norm_factor = (seq_len * lax.axis_size("fsdp") * lax.axis_size("dp")) ** (-0.5)
    weight_grad = (summed * norm_factor).astype(jnp.bfloat16)
    return (
        entropy_local.reshape(1, local_rows, QH),
        grad_local.astype(jnp.bfloat16).reshape(1, local_rows, QH * HD),
        weight_grad,
    )


def solution(mesh):
    return jax.shard_map(
        shards,
        mesh=mesh,
        in_specs=(
            P(("fsdp", "dp"), "seq", None),
            P(("fsdp", "dp"), "seq", None),
            P("fsdp", None),
            P(("fsdp", "dp"), None),
            P(("fsdp", "dp"), "seq", None),
        ),
        out_specs=(P(("fsdp", "dp"), "seq", None), P(("fsdp", "dp"), "seq", None), P("fsdp", None)),
        check_vma=False,
    )
```

profile of v0, /device:TPU:0, one launch (start us, length us, event | category | flops | bytes accessed | tf_op | source)
XLA Modules:
  0.0 553.6 jit_solution(1819505736635313049)
XLA Ops:
  8.9 107.3 %all-gather.2.cloned.1.call-done = bf16[8192,512]{1,0:T(8,128)(2,1)} async-done(((bf16[4096,512]{1,0:T(8,128)(2,1)}), bf16[8192,512]{1,0:T(8,128)(2,1)}) %all-gather.2.cloned.1.call-update) | async-done | bytes 8388624 | tf_op jit(solution)/shard_map/all_gather | solution.py:113
  116.3 7.0 %fusion.67 = bf16[256,512]{1,0:T(8,128)(2,1)S(1)} fusion(bf16[8192,512]{1,0:T(8,128)(2,1)} %all-gather.2.cloned.1.call-done, bf16[1,256,8192]{2,1,0:T(8,128)(2,1)} %param.6), kind=kOutput, calls=%fused_computation.62 | convolution fusion | flops 2147614720 | bytes 12845056 | tf_op jit(solution)/shard_map/dot_general | solution.py:111
  123.3 1.6 collective-permute-start
  124.9 3.3 copy.58
  132.4 3.6 select_reduce_fusion.3
  136.0 2.6 fusion.6
  138.7 4.5 select_reduce_fusion.2
  143.3 1.8 fusion.97
  145.2 1.8 fusion.91
  147.0 1.8 fusion.85
  148.9 1.8 fusion.103
  150.9 1.6 collective-permute-start.1
  152.5 3.9 collective-permute-done.1
  156.5 8.1 %convolution_bitcast_fusion = f32[8192,512]{0,1:T(8,128)} fusion(bf16[256,512]{0,1:T(8,128)(2,1)S(1)} %fusion.106, bf16[1,256,8192]{2,1,0:T(8,128)(2,1)S(1)} %copy-done.7), kind=kOutput, calls=%fused_computation | convolution fusion | flops 2147483648 | bytes 21233664 | tf_op jit(solution)/shard_map/dot_general | solution.py:144
  164.8 195.6 %reduce-scatter.2.cloned.1.call-done = f32[4096,512]{0,1:T(8,128)} async-done(((f32[8192,512]{0,1:T(8,128)}), f32[4096,512]{0,1:T(8,128)}) %reduce-scatter.2.cloned.1.call-update) | async-done | bytes 8388624 | tf_op jit(solution)/shard_map/reduce_scatter | solution.py:143
  360.5 0.9 copy-done.9
  361.5 4.1 fusion.58
  365.7 1.8 fusion.61
  367.9 1.8 fusion.64
  370.5 1.8 fusion.55
  372.6 2.9 copy.82
  376.2 158.1 %all-reduce.2.cloned.1.call-done = f32[4096,512]{0,1:T(8,128)} async-done(((f32[4096,512]{0,1:T(8,128)}), f32[4096,512]{0,1:T(8,128)}) %all-reduce.2.cloned.1.call-update) | async-done | bytes 8388624 | tf_op jit(solution)/shard_map/psum | solution.py:151
  534.3 6.4 %multiply_convert_fusion = bf16[4096,512]{0,1:T(8,128)(2,1)} fusion(f32[4096,512]{0,1:T(8,128)} %all-reduce.2.cloned.1.call-done), kind=kLoop, calls=%fused_computation.1 | loop fusion | flops 4194304 | bytes 12582912 | tf_op jit(solution)/shard_map/convert_element_type | solution.py:153
  540.7 6.4 %copy.83 = bf16[4096,512]{1,0:T(8,128)(2,1)} copy(bf16[4096,512]{0,1:T(8,128)(2,1)} %multiply_convert_fusion) | data formatting | bytes 8388608
  (124 shorter events, 8.7 us)
Async XLA Ops:
  7.2 109.1 %all-gather.2.cloned.1.call-start = ((), (), s32[]{:S(2)}) async-start(), calls=%async_computation.1 | async-start | bytes 12582912 | tf_op jit(solution)/shard_map/all_gather | solution.py:113
  7.9 352.5 %reduce-scatter.2.cloned.1.call-start = ((), (), s32[]{:S(2)}) async-start(), calls=%async_computation.2 | async-start | bytes 25165824 | tf_op jit(solution)/shard_map/reduce_scatter | solution.py:143
  123.3 5.0 collective-permute-start
  130.0 15.2 %copy-start.2 = (f32[512,256,8]{1,0,2:T(8,128)}, f32[512,256,8]{1,0,2:T(8,128)S(1)}, u32[]{:S(2)}) copy-start(f32[512,256,8]{1,0,2:T(8,128)S(1)} %fusion.110) | copy-start | bytes 12582916
  130.7 16.3 %copy-start = (f32[512,256,8]{1,0,2:T(8,128)}, f32[512,256,8]{1,0,2:T(8,128)S(1)}, u32[]{:S(2)}) copy-start(f32[512,256,8]{1,0,2:T(8,128)S(1)} %fusion.111) | copy-start | bytes 12582916
  131.5 17.4 %copy-start.4 = (f32[512,256,8]{1,0,2:T(8,128)}, f32[512,256,8]{1,0,2:T(8,128)S(1)}, u32[]{:S(2)}) copy-start(f32[512,256,8]{1,0,2:T(8,128)S(1)} %get-tuple-element.127) | copy-start | bytes 12582916
  132.4 16.5 %copy-start.25 = (f32[8,256]{1,0:T(8,128)}, f32[8,256]{1,0:T(8,128)S(1)}, u32[]{:S(2)}) copy-start(f32[8,256]{1,0:T(8,128)S(1)} %fusion.4) | copy-start | bytes 24580
  136.0 7.2 %copy-start.6 = (f32[512,256,8]{1,0,2:T(8,128)}, f32[512,256,8]{1,0,2:T(8,128)S(1)}, u32[]{:S(2)}) copy-start(f32[512,256,8]{1,0,2:T(8,128)S(1)} %get-tuple-element.128) | copy-start | bytes 12582916
  136.0 7.2 %copy-start.16 = (f32[8,256]{1,0:T(8,128)}, f32[8,256]{1,0:T(8,128)S(1)}, u32[]{:S(2)}) copy-start(f32[8,256]{1,0:T(8,128)S(1)} %get-tuple-element.85) | copy-start | bytes 24580
  136.0 9.1 %copy-start.10 = (f32[8,256]{1,0:T(8,128)}, f32[8,256]{1,0:T(8,128)S(1)}, u32[]{:S(2)}) copy-start(f32[8,256]{1,0:T(8,128)S(1)} %get-tuple-element.86) | copy-start | bytes 24580
  136.0 12.8 %copy-start.45 = (f32[8,256]{1,0:T(8,128)}, f32[8,256]{1,0:T(8,128)S(1)}, u32[]{:S(2)}) copy-start(f32[8,256]{1,0:T(8,128)S(1)} %get-tuple-element.84) | copy-start | bytes 24580
  138.7 4.6 copy-start.22
  138.7 6.4 %copy-start.19 = (f32[8,256]{1,0:T(8,128)}, f32[8,256]{1,0:T(8,128)S(1)}, u32[]{:S(2)}) copy-start(f32[8,256]{1,0:T(8,128)S(1)} %get-tuple-element.102) | copy-start | bytes 24580
  138.7 8.3 %copy-start.13 = (f32[8,256]{1,0:T(8,128)}, f32[8,256]{1,0:T(8,128)S(1)}, u32[]{:S(2)}) copy-start(f32[8,256]{1,0:T(8,128)S(1)} %get-tuple-element.103) | copy-start | bytes 24580
  138.7 4.6 copy-start.43
  143.2 3.8 copy-start.27
  150.7 5.8 %copy-start.7 = (bf16[1,256,8192]{2,1,0:T(8,128)(2,1)S(1)}, bf16[1,256,8192]{2,1,0:T(8,128)(2,1)}, u32[]{:S(2)}) copy-start(bf16[1,256,8192]{2,1,0:T(8,128)(2,1)} %param.6) | copy-start | bytes 12582916
  150.9 5.5 collective-permute-start.1
  164.6 369.7 %all-reduce.2.cloned.1.call-start = ((), (), s32[]{:S(2)}) async-start(), calls=%async_computation.3 | async-start | bytes 16777216 | tf_op jit(solution)/shard_map/psum | solution.py:151
  361.4 4.2 copy-start.3
  361.4 4.2 copy-start.11
  361.4 4.2 copy-start.20
  361.4 4.2 copy-start.31
  361.5 4.2 copy-start.42
  (29 other events, 64.4 us)
Sparse Core Ops, SparseCore 0:
  9.5 106.6 all-gather.1
  164.7 195.7 reduce-scatter.1
  364.2 170.0 all-reduce.1
where the time goes:
time: 554 us
  waiting for transfers between devices  466 us (84%)
  matrix products  37.5 us (7%)
  other arithmetic  16.6 us (3%)
  local copies, waits for them, and re-layouts  15.8 us (3%)
  between operations  14.6 us (3%)
    reduce_scatter x1, waiting for transfers between devices, shards(): lax.psum_scatter(lax.dot_general(columns, key_grad_low, (((0,), (0,)), ((...  196 us
    psum x1, waiting for transfers between devices, shards(): summed = lax.psum(term_rows, ('seq', 'dp'))  158 us
    all_gather x1, waiting for transfers between devices, shards(): lax.all_gather(key_weight, 'fsdp', axis=0, tiled=True)  107 us
    unnamed x99, local copies, waits for them, and re-layouts  14.9 us
  transfers between devices with their start and end apart: 5, of which 4 were waited for; matrix products, arithmetic and copies ran while one was open for 3% of the time, Pallas kernels for 0%

commit v1 on v0

--- a/solution.py
+++ b/solution.py
@@ -148,7 +148,8 @@
         scatter_dimension=0,
         tiled=True,
     )
-    summed = lax.psum(term_rows, ("seq", "dp"))
+    inner = lax.psum(term_rows, "dp")
+    summed = lax.psum(inner, "seq")
     norm_factor = (seq_len * lax.axis_size("fsdp") * lax.axis_size("dp")) ** (-0.5)
     weight_grad = (summed * norm_factor).astype(jnp.bfloat16)
     return (

time: 554 us -> 828 us (1.49)
  waiting for transfers between devices: 466 us -> 739 us
    psum x1 -> x2, waiting for transfers between devices: 158 us -> 431 us  [the longest x1 293 us: shards(): inner = lax.psum(term_rows, 'dp')]
  transfers between devices with their start and end apart: 5 -> 6, of which waited for: 4 -> 5; matrix products, arithmetic and copies ran while one was open for 3% -> 2% of each run, Pallas kernels for 0% -> 0%
where the time goes in v1:
time: 828 us; the launch traced here: 827 us
  waiting for transfers between devices  739 us (89%)
  matrix products  37.5 us (5%)
  other arithmetic  16.6 us (2%)
  local copies, waits for them, and re-layouts  16.1 us (2%)
  between operations  14.6 us (2%)
    psum x1, waiting for transfers between devices, shards(): inner = lax.psum(term_rows, 'dp')  293 us
    reduce_scatter x1, waiting for transfers between devices, shards(): lax.psum_scatter(lax.dot_general(columns, key_grad_low, (((0,), (0,)), ((...  196 us
    psum x1, waiting for transfers between devices, shards(): summed = lax.psum(inner, 'seq')  138 us
    all_gather x1, waiting for transfers between devices, shards(): lax.all_gather(key_weight, 'fsdp', axis=0, tiled=True)  107 us
  transfers between devices with their start and end apart: 6, of which 5 were waited for; matrix products, arithmetic and copies ran while one was open for 2% of the time, Pallas kernels for 0%

profile of v1, /device:TPU:0, one launch (start us, length us, event | category | flops | bytes accessed | tf_op | source)
XLA Modules:
  0.0 827.3 jit_solution(11839087837260096367)
XLA Ops:
  8.9 107.3 %all-gather.2.cloned.1.call-done = bf16[8192,512]{1,0:T(8,128)(2,1)} async-done(((bf16[4096,512]{1,0:T(8,128)(2,1)}), bf16[8192,512]{1,0:T(8,128)(2,1)}) %all-gather.2.cloned.1.call-update) | async-done | bytes 8388624 | tf_op jit(solution)/shard_map/all_gather | solution.py:113
  116.3 7.0 fusion.67
  123.3 1.6 collective-permute-start
  124.9 3.3 copy.58
  132.4 3.6 select_reduce_fusion.3
  136.0 2.6 fusion.6
  138.7 4.5 select_reduce_fusion.2
  143.3 1.8 fusion.97
  145.2 1.8 fusion.91
  147.0 1.8 fusion.85
  148.9 1.8 fusion.103
  150.9 1.6 collective-permute-start.1
  152.5 3.9 collective-permute-done.1
  156.5 8.1 convolution_bitcast_fusion
  164.6 195.8 %reduce-scatter.2.cloned.1.call-done = f32[4096,512]{0,1:T(8,128)} async-done(((f32[8192,512]{0,1:T(8,128)}), f32[4096,512]{0,1:T(8,128)}) %reduce-scatter.2.cloned.1.call-update) | async-done | bytes 8388624 | tf_op jit(solution)/shard_map/reduce_scatter | solution.py:143
  360.7 293.0 %all-reduce.3.cloned.1.call-done = f32[4096,512]{0,1:T(8,128)} async-done(((f32[4096,512]{0,1:T(8,128)}), f32[4096,512]{0,1:T(8,128)}) %all-reduce.3.cloned.1.call-update) | async-done | bytes 8388624 | tf_op jit(solution)/shard_map/psum | solution.py:151
  654.8 4.1 fusion.58
  659.0 1.8 fusion.61
  661.9 1.8 fusion.64
  664.1 1.8 fusion.55
  666.2 2.9 copy.82
  669.8 138.2 %all-reduce.5.cloned.1.call-done = f32[4096,512]{0,1:T(8,128)} async-done(((f32[4096,512]{0,1:T(8,128)}), f32[4096,512]{0,1:T(8,128)}) %all-reduce.5.cloned.1.call-update) | async-done | bytes 8388624 | tf_op jit(solution)/shard_map/psum | solution.py:152
  808.0 6.4 multiply_convert_fusion
  814.3 6.4 copy.83
  (127 shorter events, 9.9 us)
Async XLA Ops:
  7.2 109.1 %all-gather.2.cloned.1.call-start = ((), (), s32[]{:S(2)}) async-start(), calls=%async_computation.1 | async-start | bytes 12582912 | tf_op jit(solution)/shard_map/all_gather | solution.py:113
  7.9 352.5 %reduce-scatter.2.cloned.1.call-start = ((), (), s32[]{:S(2)}) async-start(), calls=%async_computation.2 | async-start | bytes 25165824 | tf_op jit(solution)/shard_map/reduce_scatter | solution.py:143
  123.3 5.0 collective-permute-start
  130.0 15.2 %copy-start.2 = (f32[512,256,8]{1,0,2:T(8,128)}, f32[512,256,8]{1,0,2:T(8,128)S(1)}, u32[]{:S(2)}) copy-start(f32[512,256,8]{1,0,2:T(8,128)S(1)} %fusion.110) | copy-start | bytes 12582916
  130.7 16.3 %copy-start = (f32[512,256,8]{1,0,2:T(8,128)}, f32[512,256,8]{1,0,2:T(8,128)S(1)}, u32[]{:S(2)}) copy-start(f32[512,256,8]{1,0,2:T(8,128)S(1)} %fusion.111) | copy-start | bytes 12582916
  131.5 17.4 %copy-start.4 = (f32[512,256,8]{1,0,2:T(8,128)}, f32[512,256,8]{1,0,2:T(8,128)S(1)}, u32[]{:S(2)}) copy-start(f32[512,256,8]{1,0,2:T(8,128)S(1)} %get-tuple-element.127) | copy-start | bytes 12582916
  132.4 16.5 %copy-start.25 = (f32[8,256]{1,0:T(8,128)}, f32[8,256]{1,0:T(8,128)S(1)}, u32[]{:S(2)}) copy-start(f32[8,256]{1,0:T(8,128)S(1)} %fusion.4) | copy-start | bytes 24580
  136.0 7.2 copy-start.6
  136.0 7.2 copy-start.16
  136.0 9.1 %copy-start.10 = (f32[8,256]{1,0:T(8,128)}, f32[8,256]{1,0:T(8,128)S(1)}, u32[]{:S(2)}) copy-start(f32[8,256]{1,0:T(8,128)S(1)} %get-tuple-element.86) | copy-start | bytes 24580
  136.0 12.8 %copy-start.45 = (f32[8,256]{1,0:T(8,128)}, f32[8,256]{1,0:T(8,128)S(1)}, u32[]{:S(2)}) copy-start(f32[8,256]{1,0:T(8,128)S(1)} %get-tuple-element.84) | copy-start | bytes 24580
  138.7 4.6 copy-start.22
  138.7 6.4 copy-start.19
  138.7 8.3 %copy-start.13 = (f32[8,256]{1,0:T(8,128)}, f32[8,256]{1,0:T(8,128)S(1)}, u32[]{:S(2)}) copy-start(f32[8,256]{1,0:T(8,128)S(1)} %get-tuple-element.103) | copy-start | bytes 24580
  138.7 4.6 copy-start.43
  150.7 5.8 copy-start.7
  150.9 5.5 collective-permute-start.1
  164.6 489.2 %all-reduce.3.cloned.1.call-start = ((), (), s32[]{:S(2)}) async-start(), calls=%async_computation.3 | async-start | bytes 16777216 | tf_op jit(solution)/shard_map/psum | solution.py:151
  360.5 447.5 %all-reduce.5.cloned.1.call-start = ((), (), s32[]{:S(2)}) async-start(), calls=%async_computation.4 | async-start | bytes 16777216 | tf_op jit(solution)/shard_map/psum | solution.py:152
  654.7 4.2 copy-start.3
  654.8 4.2 copy-start.11
  654.8 4.2 copy-start.20
  654.8 4.2 copy-start.31
  654.8 4.2 copy-start.42
  (30 other events, 69.2 us)
Sparse Core Ops, SparseCore 0:
  9.5 106.6 all-gather.1
  164.7 195.7 reduce-scatter.1
  362.9 290.8 all-reduce.2
  656.1 151.8 all-reduce.4
